TPU v7x, 32 devices: a whole 2x2x4 slice. The times are simulated.
32 devices in a mesh: groups: 2 (over y), ctx: 16 (over z, x, core).
Axes of the slice: x: 2, y: 2, z: 4, core: 2. Of those that a mesh axis runs over, the one named last changes fastest.
Arguments:
- queries: bfloat16 [32, 8192], P(('groups', 'ctx')), parts along dimension 0, may hold values from -120 to 120
- fresh_keys: bfloat16 [32, 512], P(('groups', 'ctx')), parts along dimension 0, may hold values from -4 to 4
- fresh_values: bfloat16 [32, 512], P(('groups', 'ctx')), parts along dimension 0, may hold values from -4 to 4
- cache_keys: bfloat16 [32768, 512], P(('groups', 'ctx')), parts along dimension 0, may hold values from -4 to 4
- stored_values: bfloat16 [32768, 512], P(('groups', 'ctx')), parts along dimension 0, may hold values from -4 to 4
- cache_lengths: int32 [32], P(('groups', 'ctx')), parts along dimension 0, may hold values from 1 to 1024, as said below
- positions: int32 [32], P('groups'), parts along dimension 0, may hold values from 0 to 15, each once
Outputs:
- attended: bfloat16 [32, 8192], P(('groups', 'ctx')), parts along dimension 0
There are 2 independent parts, one for each index of `groups`. A program takes and returns all parts, laid end to end along the dimension named above; each array names one. Nothing has to cross between parts.
Inputs may be any that keep to these rules, and one draw needn't show every extreme that they name: `cache_lengths`: each entry lies between 1 and 1024, and one shard has all 1024 slots live.
All inputs are finite; a program needn't handle non-finite values.
Results may differ from a plain program's by a relative error of at most 0.003.
Values may be sent and summed in bfloat16 or wider, within the bound.
A program may use at most 128 MiB of HBM per device.

v0:
```python
import jax
import jax.numpy as jnp
from jax import lax
from jax.sharding import PartitionSpec as P

HEADS_PER_GROUP = 16
HEAD_WIDTH = 128


def body(queries, fresh_keys, fresh_values, cache_keys, stored_values, cache_lengths, positions):
    device_rank = lax.axis_index("ctx")
    new_rows = fresh_keys.shape[0]
    cache_rows = cache_keys.shape[0]
    head_size = HEAD_WIDTH
    group_size = HEADS_PER_GROUP
    kv_heads = fresh_keys.shape[1] // head_size
    query_heads = kv_heads * group_size
    all_keys = jnp.concatenate([cache_keys, fresh_keys], axis=0)
    all_values = jnp.concatenate([stored_values, fresh_values], axis=0)
    gathered = lax.all_gather(queries, "ctx", axis=0, tiled=True)
    total_new = gathered.shape[0]
    key_order = lax.dynamic_slice_in_dim(positions, device_rank * new_rows, new_rows, 0)
    live = jnp.arange(cache_rows, dtype=jnp.int32) < cache_lengths[0]
    cache_seen = jnp.broadcast_to(live[None, :], (total_new, cache_rows))
    new_seen = key_order[None, :] <= positions[:, None]
    visible = jnp.concatenate([cache_seen, new_seen], axis=1)
    maxima_list = []
    totals_list = []
    sums_list = []
    for head_group in range(kv_heads):
        query_part = gathered[
            :, head_group * group_size * head_size : (head_group + 1) * group_size * head_size
        ].reshape(total_new, group_size, head_size)
        key_part = all_keys[:, head_group * head_size : (head_group + 1) * head_size]
        value_part = all_values[:, head_group * head_size : (head_group + 1) * head_size]
        scores = jnp.einsum(
            "ngd,kd->ngk", query_part, key_part, preferred_element_type=jnp.float32
        ) * head_size ** (-0.5)
        scores = jnp.where(visible[:, None, :], scores, -jnp.inf)
        maxima = jnp.max(scores, axis=-1)
        weights = jnp.exp(scores - maxima[..., None]).astype(jnp.bfloat16)
        totals = jnp.sum(weights.astype(jnp.float32), axis=-1)
        sums = jnp.einsum("ngk,kd->ngd", weights, value_part, preferred_element_type=jnp.float32)
        maxima_list.append(maxima)
        totals_list.append(totals)
        sums_list.append(sums.reshape(total_new, group_size * head_size))
    block_max = jnp.concatenate(maxima_list, axis=1)
    block_total = jnp.concatenate(totals_list, axis=1)
    block_sum = jnp.concatenate(sums_list, axis=1)
    sums_in, maxima_in, totals_in = (
        lax.all_to_all(block_sum[None], "ctx", split_axis=1, concat_axis=0, tiled=True),
        lax.all_to_all(block_max[None], "ctx", split_axis=1, concat_axis=0, tiled=True),
        lax.all_to_all(block_total[None], "ctx", split_axis=1, concat_axis=0, tiled=True),
    )
    overall = jnp.max(maxima_in, axis=0)
    scale = jnp.exp(maxima_in - overall[None])
    sources = sums_in.shape[0]
    numerator = jnp.sum(
        sums_in.reshape(sources, new_rows, query_heads, head_size) * scale[..., None], axis=0
    )
    denominator = jnp.sum(totals_in * scale, axis=0)
    result = numerator / denominator[..., None]
    return result.reshape(new_rows, query_heads * head_size).astype(jnp.bfloat16)


def solution(mesh):
    return jax.shard_map(
        body,
        mesh=mesh,
        in_specs=(
            P(("groups", "ctx"), None),
            P(("groups", "ctx"), None),
            P(("groups", "ctx"), None),
            P(("groups", "ctx"), None),
            P(("groups", "ctx"), None),
            P(("groups", "ctx")),
            P("groups"),
        ),
        out_specs=P(("groups", "ctx"), None),
        check_vma=False,
    )
```

profile of v0, /device:TPU:0, one launch (start us, length us, event | category | flops | bytes accessed | tf_op | source)
XLA Modules:
  0.0 74.4 jit_solution(8473984056943046898)
XLA Ops:
  0.7 1.2 %dynamic_slice.3 = s32[1]{0:T(128)} dynamic-slice(s32[16]{0:T(128)} %param.13, s32[]{:T(128)S(6)} %select_n.16), dynamic_slice_sizes={1} | dynamic-slice | bytes 12 | tf_op jit(solution)/shard_map/dynamic_slice | solution.py:22
  1.9 1.3 %compare_bitcast_fusion = pred[16,1]{0,1:T(4,128)(4,1)S(1)} fusion(s32[16]{0:T(128)} %param.13, s32[]{:T(128)} %bitcast.1), kind=kLoop, calls=%fused_computation.57 | loop fusion | flops 16 | bytes 84 | tf_op jit(solution)/shard_map/le | solution.py:25
  3.2 0.1 copy.10
  3.3 24.9 %all-gather = bf16[16,1,8192]{2,1,0:T(2,128)(2,1)S(1)} all-gather(bf16[1,1,8192]{2,1,0:T(2,128)(2,1)} %bitcast.115), channel_id=1, replica_groups=mesh['groups'=2,'ctx'=16] {'ctx'}, dimensions={0}, use_global_device_ids=true | all-gather | bytes 278528 | tf_op jit(solution)/shard_map/all_gather | solution.py:20
  28.2 0.3 copy.25
  28.6 0.0 copy-start.6
  28.7 0.0 copy-done.1
  28.7 0.1 constant_dynamic-update-slice_fusion.1
  28.8 0.5 copy-done.6
  29.3 0.4 fusion.15
  29.7 0.4 fusion.16
  30.2 0.0 copy-start.2
  30.2 0.4 fusion.17
  30.6 1.4 %fusion.18 = (f32[16,16]{1,0:T(8,128)S(1)}, f32[16,16,1025]{2,1,0:T(8,128)}) fusion(bf16[16,16,128]{2,1,0:T(8,128)(2,1)S(1)} %bitcast.105, bf16[1025,512]{1,0:T(8,128)(2,1)S(1)} %constant_dynamic-update-slice_fusion, pred[16,1025]{1,0:T(8,128)(4,1)S(1)} %pad_add_fusion), kind=kOutput, calls=%fused_computation.61 | convolution fusion | flops 67961344 | bytes 1398784 | tf_op jit(solution)/shard_map/ngd,kd->ngk/dot_general | solution.py:36
  32.0 0.0 copy-done.2
  32.0 0.7 pad_maximum_fusion.1
  32.6 0.0 copy-done.4
  32.6 4.1 %all-to-all-start.1 = ((f32[1,16,64]{2,0,1:T(1,128)}), f32[1,16,64]{2,0,1:T(1,128)}, u32[]{:S(2)}, u32[]{:S(2)}) async-start(f32[1,16,64]{2,0,1:T(1,128)} %bitcast.116), calls=%async_computation.1 | async-start | bytes 16384 | tf_op jit(solution)/shard_map/all_to_all | solution.py:52
  36.7 0.0 copy-start.7
  36.7 1.3 %constant_dynamic-update-slice_fusion.3 = bf16[1025,512]{1,0:T(8,128)(2,1)S(1)} fusion(bf16[1024,512]{1,0:T(8,128)(2,1)} %param.11), kind=kLoop, calls=%fused_computation.48 | loop fusion | bytes 2097152
  38.0 0.0 copy-done.7
  38.1 0.0 copy-start.3
  38.1 0.4 fusion.8
  38.5 0.3 copy-done.3
  38.8 0.5 convert_reduce_fusion
  39.2 0.0 copy-start
  39.2 0.0 copy-start.5
  39.2 0.4 fusion.9
  39.6 0.9 %copy-done = f32[16,16,1025]{2,1,0:T(8,128)S(1)} copy-done((f32[16,16,1025]{2,1,0:T(8,128)S(1)}, f32[16,16,1025]{2,1,0:T(8,128)}, u32[]{:S(2)}) %copy-start) | copy-done | bytes 1049624
  40.5 0.4 fusion.11
  40.9 0.5 convert_reduce_fusion.2
  41.4 0.4 fusion.10
  41.7 0.1 copy_bitcast_fusion.1
  41.8 0.1 copy_bitcast_fusion.3
  41.9 0.7 pad_maximum_fusion.2
  42.6 0.6 all-to-all-done.1
  43.2 5.4 %all-to-all-start.2 = ((f32[1,16,64]{2,0,1:T(1,128)}), f32[1,16,64]{2,0,1:T(1,128)S(1)}, u32[]{:S(2)}, u32[]{:S(2)}) async-start(f32[1,16,64]{2,0,1:T(1,128)} %bitcast.20), calls=%async_computation.2 | async-start | bytes 16384 | tf_op jit(solution)/shard_map/all_to_all | solution.py:53
  48.6 1.3 %broadcast_in_dim.55 = f32[1,16,8192]{2,0,1:T(1,128)} reshape(f32[16,8192]{1,0:T(8,128)S(1)} %pad_maximum_fusion) | data formatting | bytes 1048576 | tf_op jit(solution)/shard_map/broadcast_in_dim | solution.py:51
  49.9 5.0 %all-to-all-done.2 = f32[1,16,64]{2,0,1:T(1,128)S(1)} async-done(((f32[1,16,64]{2,0,1:T(1,128)}), f32[1,16,64]{2,0,1:T(1,128)S(1)}, u32[]{:S(2)}, u32[]{:S(2)}) %all-to-all-start.2) | async-done | bytes 4128 | tf_op jit(solution)/shard_map/all_to_all | solution.py:53
  54.9 3.6 %all-to-all-start = ((f32[1,16,8192]{2,0,1:T(1,128)}), f32[1,16,8192]{2,0,1:T(1,128)S(1)}, u32[]{:S(2)}, u32[]{:S(2)}) async-start(f32[1,16,8192]{2,0,1:T(1,128)} %broadcast_in_dim.55), calls=%async_computation | async-start | bytes 1048576 | tf_op jit(solution)/shard_map/all_to_all | solution.py:51
  58.5 0.7 reduce_max.49
  59.2 0.7 fusion.14
  59.9 0.7 subtract_exponential_fusion
  60.6 12.1 %all-to-all-done = f32[1,16,8192]{2,0,1:T(1,128)S(1)} async-done(((f32[1,16,8192]{2,0,1:T(1,128)}), f32[1,16,8192]{2,0,1:T(1,128)S(1)}, u32[]{:S(2)}, u32[]{:S(2)}) %all-to-all-start) | async-done | bytes 524320 | tf_op jit(solution)/shard_map/all_to_all | solution.py:51
  72.7 0.2 mul.59
  72.9 0.8 %multiply_reduce_fusion = f32[8192]{0:T(1024)S(1)} fusion(f32[1,16,8192]{2,0,1:T(1,128)S(1)} %all-to-all-done, f32[1,16,8192]{2,0,1:T(1,128)S(1)} %bitcast.103), kind=kLoop, calls=%fused_computation.21 | loop fusion | flops 253952 | bytes 1081344 | tf_op jit(solution)/shard_map/reduce_sum | solution.py:58
  73.7 0.1 div.20
  73.7 0.7 divide_convert_fusion
  (14 shorter events, 0.2 us)
Async XLA Ops:
  3.3 25.4 %copy-start.1 = (bf16[1024,512]{1,0:T(8,128)(2,1)S(1)}, bf16[1024,512]{1,0:T(8,128)(2,1)}, u32[]{:S(2)}) copy-start(bf16[1024,512]{1,0:T(8,128)(2,1)} %param.10) | copy-start | bytes 3145732
  28.6 0.7 copy-start.6
  30.2 1.8 %copy-start.2 = (f32[16,16]{1,0:T(8,128)}, f32[16,16]{1,0:T(8,128)S(1)}, u32[]{:S(2)}) copy-start(f32[16,16]{1,0:T(8,128)S(1)} %get-tuple-element.11) | copy-start | bytes 3076
  32.0 0.7 copy-start.4
  32.6 10.5 %all-to-all-start.1 = ((f32[1,16,64]{2,0,1:T(1,128)}), f32[1,16,64]{2,0,1:T(1,128)}, u32[]{:S(2)}, u32[]{:S(2)}) async-start(f32[1,16,64]{2,0,1:T(1,128)} %bitcast.116), calls=%async_computation.1 | async-start | bytes 16384 | tf_op jit(solution)/shard_map/all_to_all | solution.py:52
  36.7 1.3 %copy-start.7 = (bf16[1,512]{1,0:T(2,128)(2,1)S(1)}, bf16[1,512]{1,0:T(2,128)(2,1)}, u32[]{:S(2)}) copy-start(bf16[1,512]{1,0:T(2,128)(2,1)} %param.9) | copy-start | bytes 3076
  38.1 0.7 copy-start.3
  39.2 1.3 %copy-start = (f32[16,16,1025]{2,1,0:T(8,128)S(1)}, f32[16,16,1025]{2,1,0:T(8,128)}, u32[]{:S(2)}) copy-start(f32[16,16,1025]{2,1,0:T(8,128)} %get-tuple-element.16) | copy-start | bytes 3148804
  39.2 1.3 %copy-start.5 = (f32[16,16]{1,0:T(8,128)S(1)}, f32[16,16]{1,0:T(8,128)}, u32[]{:S(2)}) copy-start(f32[16,16]{1,0:T(8,128)} %copy-done.4) | copy-start | bytes 3076
  43.2 11.7 %all-to-all-start.2 = ((f32[1,16,64]{2,0,1:T(1,128)}), f32[1,16,64]{2,0,1:T(1,128)S(1)}, u32[]{:S(2)}, u32[]{:S(2)}) async-start(f32[1,16,64]{2,0,1:T(1,128)} %bitcast.20), calls=%async_computation.2 | async-start | bytes 16384 | tf_op jit(solution)/shard_map/all_to_all | solution.py:53
  54.9 17.8 %all-to-all-start = ((f32[1,16,8192]{2,0,1:T(1,128)}), f32[1,16,8192]{2,0,1:T(1,128)S(1)}, u32[]{:S(2)}, u32[]{:S(2)}) async-start(f32[1,16,8192]{2,0,1:T(1,128)} %broadcast_in_dim.55), calls=%async_computation | async-start | bytes 1048576 | tf_op jit(solution)/shard_map/all_to_all | solution.py:51
where the time goes:
time: 75 us; the launch traced here: 74.4 us
  blocking collectives  24.9 us (33%)
  waiting for transfers between devices  17.6 us (23%)
  starting transfers between devices  13 us (17%)
  other arithmetic  7.23 us (10%)
  local copies, waits for them, and re-layouts  6.58 us (9%)
  matrix products  4.12 us (5%)
  between operations  0.93 us (1%)
    all_gather x1, blocking collectives, body(): gathered = lax.all_gather(queries, 'ctx', axis=0, tiled=True)  24.9 us
    all_to_all x1, waiting for transfers between devices, body(): lax.all_to_all(block_sum[None], 'ctx', split_axis=1, concat_axis=0, tiled...  12.1 us
    all_to_all x1, starting transfers between devices, body(): lax.all_to_all(block_total[None], 'ctx', split_axis=1, concat_axis=0, til...  5.35 us
    all_to_all x1, waiting for transfers between devices, body(): lax.all_to_all(block_total[None], 'ctx', split_axis=1, concat_axis=0, til...  4.99 us
    all_to_all x1, starting transfers between devices, body(): lax.all_to_all(block_max[None], 'ctx', split_axis=1, concat_axis=0, tiled...  4.08 us
    all_to_all x1, starting transfers between devices, body(): lax.all_to_all(block_sum[None], 'ctx', split_axis=1, concat_axis=0, tiled...  3.57 us
    unnamed x24, local copies, waits for them, and re-layouts  3.45 us
    dot_general x4, matrix products, body(): jnp.einsum('ngd,kd->ngk', query_part, key_part, preferred_element_type=jn...  2.63 us
  transfers between devices with their start and end apart: 3, of which 3 were waited for; matrix products, arithmetic and copies ran while one was open for 11% of the time, Pallas kernels for 0%

commit v1 on v0

v1 whole, which is shorter than its diff:
```python
import functools
import math

import jax
import jax.numpy as jnp
from jax import lax
from jax.experimental import pallas as pl
from jax.experimental.pallas import tpu as pltpu
from jax.sharding import PartitionSpec as P

HEADS_PER_GROUP = 16
HEAD_WIDTH = 128
MESH = pl.DeviceIdType.MESH


def partner(rank, step, count):
    if count & (count - 1) == 0:
        return rank ^ step
    return lax.rem(rank + step, count)


def source(rank, step, count):
    if count & (count - 1) == 0:
        return rank ^ step
    return lax.rem(rank + count - step, count)


def kernel(n, chunk, lengths_ref, positions_ref, q_ref, fk_ref, fv_ref, keys_hbm, values_hbm, out_ref,
           keys, values, q_all, sums, stats, sums_in, stats_in,
           kv_sem, q_send, q_recv, s_send, s_recv, t_send, t_recv):
    me = lax.axis_index("ctx")
    cache_rows = keys.shape[0]
    heads = q_ref.shape[0]
    width = HEAD_WIDTH
    group = HEADS_PER_GROUP
    kv_heads = heads // group
    factor = width ** -0.5 * math.log2(math.e)

    key_copy = pltpu.make_async_copy(keys_hbm, keys, kv_sem.at[0])
    value_copy = pltpu.make_async_copy(values_hbm, values, kv_sem.at[1])
    key_copy.start()
    value_copy.start()

    barrier = pltpu.get_barrier_semaphore()

    @pl.loop(1, n)
    def _(step):
        pl.semaphore_signal(barrier, inc=1, device_id={"ctx": partner(me, step, n)}, device_id_type=MESH)

    pl.semaphore_wait(barrier, n - 1)

    def q_copy(peer):
        return pltpu.make_async_remote_copy(
            src_ref=q_ref, dst_ref=q_all.at[me], send_sem=q_send.at[peer], recv_sem=q_recv.at[me],
            device_id={"ctx": peer}, device_id_type=MESH)

    def q_arrival(peer):
        return pltpu.make_async_remote_copy(
            src_ref=q_ref, dst_ref=q_all.at[peer], send_sem=q_send.at[peer], recv_sem=q_recv.at[peer],
            device_id={"ctx": peer}, device_id_type=MESH)

    @pl.loop(1, n)
    def _(step):
        q_copy(partner(me, n - step, n)).start()

    q_all[me] = q_ref[...]

    key_copy.wait()
    value_copy.wait()

    dead = jnp.where(
        lax.broadcasted_iota(jnp.int32, (1, cache_rows), 1) < lengths_ref[0], 0.0, -jnp.inf
    ).astype(jnp.float32)
    lane = lax.broadcasted_iota(jnp.int32, (group, width), 1)
    row = lax.broadcasted_iota(jnp.int32, (group, width), 0)
    ones = jnp.ones((cache_rows, width), jnp.bfloat16)
    own_order = positions_ref[me]
    n_chunks = n // chunk
    my_chunk = me // chunk

    def sums_copy(peer):
        return pltpu.make_async_remote_copy(
            src_ref=sums.at[peer], dst_ref=sums_in.at[me], send_sem=s_send.at[peer], recv_sem=s_recv.at[me],
            device_id={"ctx": peer}, device_id_type=MESH)

    def stats_copy(peer):
        return pltpu.make_async_remote_copy(
            src_ref=stats.at[peer], dst_ref=stats_in.at[me], send_sem=t_send.at[peer], recv_sem=t_recv.at[me],
            device_id={"ctx": peer}, device_id_type=MESH)

    def process(base):
        fresh_bias = jnp.concatenate(
            [jnp.full((group, 1), jnp.where(own_order <= positions_ref[base + i], 0.0, -jnp.inf), jnp.float32)
             for i in range(chunk)], axis=0)
        packed = [jnp.zeros((group, width), jnp.float32) for _ in range(chunk)]
        for h in range(kv_heads):
            cols = slice(h * width, (h + 1) * width)
            q = q_all[pl.ds(base, chunk), h * group:(h + 1) * group, :].reshape(chunk * group, width)
            s = lax.dot_general(q, keys[:, cols], (((1,), (1,)), ((), ())),
                                preferred_element_type=jnp.float32) + dead
            fk = fk_ref[:, cols].astype(jnp.float32)
            fv = fv_ref[:, cols].astype(jnp.float32)
            sf = jnp.sum(q.astype(jnp.float32) * fk, axis=1, keepdims=True) + fresh_bias
            m = jnp.maximum(jnp.max(s, axis=1, keepdims=True), sf)
            p = jnp.exp2((s - m) * factor).astype(jnp.bfloat16)
            pf = jnp.exp2((sf - m) * factor).astype(jnp.bfloat16).astype(jnp.float32)
            o = jnp.dot(p, jnp.concatenate([values[:, cols], ones], axis=1), preferred_element_type=jnp.float32)
            total = o[:, width:] + pf
            block = o[:, :width] + pf * fv
            sums[pl.ds(base, chunk), h * group:(h + 1) * group, :] = block.astype(jnp.bfloat16).reshape(
                chunk, group, width)
            for i in range(chunk):
                part = slice(i * group, (i + 1) * group)
                packed[i] = jnp.where(lane == row + h * group, m[part], packed[i])
                packed[i] = jnp.where(lane == row + h * group + heads, total[part], packed[i])
        for i in range(chunk):
            stats[base + i] = jnp.sum(packed[i], axis=0, keepdims=True)

    @pl.loop(0, n_chunks)
    def _(step):
        base = source(my_chunk, step, n_chunks) * chunk

        @pl.loop(0, chunk)
        def _(i):
            @pl.when(base + i != me)
            def _():
                q_arrival(base + i).wait_recv()

        process(base)

        @pl.loop(0, chunk)
        def _(i):
            @pl.when(base + i != me)
            def _():
                stats_copy(base + i).start()
                sums_copy(base + i).start()

    stats_in[me] = stats[me]
    sums_in[me] = sums[me]

    @pl.loop(1, n)
    def _(step):
        peer = partner(me, step, n)
        pltpu.make_async_remote_copy(
            src_ref=stats.at[peer], dst_ref=stats_in.at[peer], send_sem=t_send.at[peer], recv_sem=t_recv.at[peer],
            device_id={"ctx": peer}, device_id_type=MESH).wait_recv()

    st = stats_in[...].reshape(n, width)
    coef = jnp.exp2((st - jnp.max(st, axis=0, keepdims=True)) * factor)
    den = jnp.sum(coef * pltpu.roll(st, width - heads, 1), axis=0, keepdims=True)
    w = coef / den
    if n < width:
        w = jnp.concatenate([w, jnp.zeros((width - n, width), jnp.float32)], axis=0)
    w = w.T

    @pl.loop(1, n)
    def _(step):
        peer = partner(me, step, n)
        pltpu.make_async_remote_copy(
            src_ref=sums.at[peer], dst_ref=sums_in.at[peer], send_sem=s_send.at[peer], recv_sem=s_recv.at[peer],
            device_id={"ctx": peer}, device_id_type=MESH).wait_recv()

    result = jnp.zeros((heads, width), jnp.float32)
    for b in range(n):
        result += w[:heads, b:b + 1] * sums_in[b].astype(jnp.float32)
    out_ref[...] = result.astype(jnp.bfloat16)

    @pl.loop(1, n)
    def _(step):
        peer = partner(me, step, n)
        q_copy(peer).wait_send()
        stats_copy(peer).wait_send()
        sums_copy(peer).wait_send()


def body(n, queries, fresh_keys, fresh_values, cache_keys, stored_values, cache_lengths, positions):
    rows = queries.shape[0]
    assert rows == 1
    heads = queries.shape[1] // HEAD_WIDTH
    cache_rows, kv_width = cache_keys.shape
    vmem = pl.BlockSpec(memory_space=pltpu.VMEM)
    smem = pl.BlockSpec(memory_space=pltpu.SMEM)
    hbm = pl.BlockSpec(memory_space=pl.ANY)
    chunk = 4 if n % 4 == 0 else 1
    block = (n, heads, HEAD_WIDTH)
    dma = pltpu.SemaphoreType.DMA
    out = pl.pallas_call(
        functools.partial(kernel, n, chunk),
        out_shape=jax.ShapeDtypeStruct((heads, HEAD_WIDTH), jnp.bfloat16),
        in_specs=[smem, smem, vmem, vmem, vmem, hbm, hbm],
        out_specs=vmem,
        scratch_shapes=[
            pltpu.VMEM((cache_rows, kv_width), jnp.bfloat16),
            pltpu.VMEM((cache_rows, kv_width), jnp.bfloat16),
            pltpu.VMEM(block, jnp.bfloat16),
            pltpu.VMEM(block, jnp.bfloat16),
            pltpu.VMEM((n, 1, HEAD_WIDTH), jnp.float32),
            pltpu.VMEM(block, jnp.bfloat16),
            pltpu.VMEM((n, 1, HEAD_WIDTH), jnp.float32),
            dma((2,)), dma((n,)), dma((n,)), dma((n,)), dma((n,)), dma((n,)), dma((n,)),
        ],
        compiler_params=pltpu.CompilerParams(collective_id=0, has_side_effects=True),
    )(cache_lengths, positions, queries.reshape(heads, HEAD_WIDTH), fresh_keys, fresh_values,
      cache_keys, stored_values)
    return out.reshape(rows, heads * HEAD_WIDTH)


def solution(mesh):
    return jax.shard_map(
        functools.partial(body, mesh.shape["ctx"]),
        mesh=mesh,
        in_specs=(
            P(("groups", "ctx"), None),
            P(("groups", "ctx"), None),
            P(("groups", "ctx"), None),
            P(("groups", "ctx"), None),
            P(("groups", "ctx"), None),
            P(("groups", "ctx")),
            P("groups"),
        ),
        out_specs=P(("groups", "ctx"), None),
        check_vma=False,
    )
```

time: 75 us -> 27 us (0.36)
  blocking collectives: 24.9 us -> 0 us
  Pallas kernels: 0 us -> 23.2 us
  waiting for transfers between devices: 17.6 us -> 0 us
  starting transfers between devices: 13 us -> 0 us
  other arithmetic: 7.23 us -> 1.45 us
  local copies, waits for them, and re-layouts: 6.58 us -> 1.36 us
  matrix products: 4.12 us -> 0 us
    all_gather x1 -> x0, blocking collectives: 24.9 us -> none  [body(): gathered = lax.all_gather(queries, 'ctx', axis=0, tiled=True)]
    pallas_call x0 -> x1, Pallas kernels: none -> 23.2 us  [body(): pl.pallas_call(functools.partial(kernel, n, chunk), out_shape=jax.ShapeDt...]
    all_to_all x3 -> x0, waiting for transfers between devices: 17.6 us -> none  [the longest x1 12.1 us: body(): lax.all_to_all(block_sum[None], 'ctx', split_axis=1, concat_axis=0, tiled...]
    all_to_all x3 -> x0, starting transfers between devices: 13 us -> none  [the longest x1 5.35 us: body(): lax.all_to_all(block_total[None], 'ctx', split_axis=1, concat_axis=0, til...]
    dot_general x8 -> x0, matrix products: 4.12 us -> none  [the longest x4 2.63 us: body(): jnp.einsum('ngd,kd->ngk', query_part, key_part, preferred_element_type=jn...]
    reduce_sum x4 -> x0, other arithmetic: 2.42 us -> none  [the longest x2 0.94 us: body(): totals = jnp.sum(weights.astype(jnp.float32), axis=-1)]
    unnamed x24 -> x1, local copies, waits for them, and re-layouts: 3.45 us -> 1.36 us
    unnamed x0 -> x1, other arithmetic: none -> 1.45 us
  transfers between devices with their start and end apart: 3 -> 0, of which waited for: 3 -> 0; matrix products, arithmetic and copies ran while one was open for 11% -> 0% of each run, Pallas kernels for 0% -> 0%
where the time goes in v1:
time: 27 us; the launch traced here: 26.7 us
  Pallas kernels  23.2 us (86%)
  other arithmetic  1.45 us (5%)
  local copies, waits for them, and re-layouts  1.36 us (5%)
  between operations  0.66 us (2%)
    pallas_call x1, Pallas kernels, body(): pl.pallas_call(functools.partial(kernel, n, chunk), out_shape=jax.ShapeDt...  23.2 us
    unnamed x1, other arithmetic  1.45 us
    unnamed x1, local copies, waits for them, and re-layouts  1.36 us

profile of v1, /device:TPU:0, one launch (start us, length us, event | category | flops | bytes accessed | tf_op | source)
XLA Modules:
  0.0 26.7 jit_solution(1429095785921956810)
XLA Ops:
  0.7 1.5 %reduce = bf16[8192]{0:T(1024)(128)(2,1)} reduce(bf16[1,8192]{1,0:T(2,128)(2,1)} %param.7, bf16[]{:T(256)} %constant.4), dimensions={0}, to_apply=%param.7.reduce_sub_computation | reduce | bytes 32770 | tf_op args[0]
  2.1 23.2 %shard_map.73 = bf16[64,128]{1,0:T(8,128)(2,1)} custom-call(s32[1]{0:T(128)S(6)} %copy.11.lengths_ref, s32[16]{0:T(128)} %positions_ref.1, bf16[64,128]{1,0:T(8,128)(2,1)} %bitcast.6, bf16[1,512]{1,0:T(2,128)(2,1)} %fk_ref.1, bf16[1,512]{1,0:T(2,128)(2,1)} %fv_ref.1, bf16[1024,512]{1,0:T(8,128)(2,1)} %keys_hbm.1, bf16[1024,512]{1,0:T(8,128)(2,1)} %values_hbm.1), custom_call_target="tpu_custom_call" | custom-call | tf_op jit(solution)/shard_map/pallas_call | solution.py:187
  25.4 1.4 %copy.10 = bf16[1,1,64,128]{3,1,2,0:T(2,128)(2,1)} copy(bf16[1,1,64,128]{3,2,1,0:T(8,128)(2,1)} %bitcast.7) | data formatting | bytes 32768

commit v2 on v1

v2 whole, which is shorter than its diff:
```python
import functools
import math

import jax
import jax.numpy as jnp
from jax import lax
from jax.experimental import pallas as pl
from jax.experimental.pallas import tpu as pltpu
from jax.sharding import PartitionSpec as P

HEADS_PER_GROUP = 16
HEAD_WIDTH = 128
MESH = pl.DeviceIdType.MESH


def kernel(n, chunk, queries_hbm, fresh_keys_hbm, fresh_values_hbm, keys_hbm, values_hbm, lengths_hbm, positions_hbm,
           out_ref, keys, values, q_row, fk_ref, fv_ref, lengths_ref, positions_ref,
           q_all, sums, stats, sums_in, stats_in,
           load_sem, q_send, q_recv, s_send, s_recv, t_send, t_recv):
    me = lax.axis_index("ctx")
    cache_rows = keys.shape[0]
    heads = q_all.shape[1]
    width = HEAD_WIDTH
    group = HEADS_PER_GROUP
    kv_heads = heads // group
    factor = width ** -0.5 * math.log2(math.e)
    line = n // chunk
    beside, across = me ^ 1, me ^ 2

    loads = [
        pltpu.make_async_copy(src, dst, load_sem.at[i])
        for i, (src, dst) in enumerate([
            (queries_hbm, q_row), (keys_hbm, keys), (values_hbm, values), (fresh_keys_hbm, fk_ref),
            (fresh_values_hbm, fv_ref), (lengths_hbm, lengths_ref), (positions_hbm, positions_ref)])
    ]
    for load in loads:
        load.start()

    barrier = pltpu.get_barrier_semaphore()
    pl.semaphore_signal(barrier, inc=1, device_id={"ctx": beside}, device_id_type=MESH)
    pl.semaphore_signal(barrier, inc=1, device_id={"ctx": across}, device_id_type=MESH)

    @pl.loop(1, line)
    def _(t):
        pl.semaphore_signal(barrier, inc=1, device_id={"ctx": me ^ (t * chunk)}, device_id_type=MESH)

    loads[0].wait()
    q_all[me] = q_row[...].astype(jnp.float32).reshape(heads, width).astype(jnp.bfloat16)
    pl.semaphore_wait(barrier, line + 1)

    def q_copy(row, peer, slot):
        return pltpu.make_async_remote_copy(
            src_ref=q_all.at[row], dst_ref=q_all.at[row], send_sem=q_send.at[slot], recv_sem=q_recv.at[row],
            device_id={"ctx": peer}, device_id_type=MESH)

    def to_line(t):
        return q_copy(me, me ^ (t * chunk), t)

    def to_across(t):
        return q_copy(me ^ (t * chunk), across, line + t)

    def to_beside(t, far):
        return q_copy((across if far else me) ^ (t * chunk), beside, (2 + far) * line + t)

    def arrive(row):
        q_copy(row, beside, 0).wait_recv()

    @pl.loop(1, line)
    def _(t):
        to_line(line - t).start()

    to_across(0).start()
    to_beside(0, 0).start()

    @pl.loop(1, line)
    def _(t):
        arrive(me ^ (t * chunk))
        to_across(t).start()
        to_beside(t, 0).start()
        arrive(across ^ ((t - 1) * chunk))
        to_beside(t - 1, 1).start()

    def last_across():
        arrive(across ^ ((line - 1) * chunk))
        to_beside(line - 1, 1).start()

    for load in loads[1:]:
        load.wait()

    dead = jnp.where(
        lax.broadcasted_iota(jnp.int32, (1, cache_rows), 1) < lengths_ref[0], 0.0, -jnp.inf
    ).astype(jnp.float32)
    lane = lax.broadcasted_iota(jnp.int32, (group, width), 1)
    row = lax.broadcasted_iota(jnp.int32, (group, width), 0)
    ones = jnp.ones((cache_rows, width), jnp.bfloat16)
    own_order = positions_ref[me]
    if line == 1:
        last_across()

    def sums_copy(peer):
        return pltpu.make_async_remote_copy(
            src_ref=sums.at[peer], dst_ref=sums_in.at[me], send_sem=s_send.at[peer], recv_sem=s_recv.at[me],
            device_id={"ctx": peer}, device_id_type=MESH)

    def stats_copy(peer):
        return pltpu.make_async_remote_copy(
            src_ref=stats.at[peer], dst_ref=stats_in.at[me], send_sem=t_send.at[peer], recv_sem=t_recv.at[me],
            device_id={"ctx": peer}, device_id_type=MESH)

    def process(base):
        fresh_bias = jnp.concatenate(
            [jnp.full((group, 1), jnp.where(own_order <= positions_ref[base + i], 0.0, -jnp.inf), jnp.float32)
             for i in range(chunk)], axis=0)
        packed = [jnp.zeros((group, width), jnp.float32) for _ in range(chunk)]
        for h in range(kv_heads):
            cols = slice(h * width, (h + 1) * width)
            q = q_all[pl.ds(base, chunk), h * group:(h + 1) * group, :].reshape(chunk * group, width)
            s = lax.dot_general(q, keys[:, cols], (((1,), (1,)), ((), ())),
                                preferred_element_type=jnp.float32) + dead
            fk = fk_ref[:, cols].astype(jnp.float32)
            fv = fv_ref[:, cols].astype(jnp.float32)
            sf = jnp.sum(q.astype(jnp.float32) * fk, axis=1, keepdims=True) + fresh_bias
            m = jnp.maximum(jnp.max(s, axis=1, keepdims=True), sf)
            p = jnp.exp2((s - m) * factor).astype(jnp.bfloat16)
            pf = jnp.exp2((sf - m) * factor).astype(jnp.bfloat16).astype(jnp.float32)
            o = jnp.dot(p, jnp.concatenate([values[:, cols], ones], axis=1), preferred_element_type=jnp.float32)
            total = o[:, width:] + pf
            block = (o[:, :width] + pf * fv) / total
            sums[pl.ds(base, chunk), h * group:(h + 1) * group, :] = block.astype(jnp.bfloat16).reshape(
                chunk, group, width)
            for i in range(chunk):
                part = slice(i * group, (i + 1) * group)
                packed[i] = jnp.where(lane == row + h * group, m[part], packed[i])
                packed[i] = jnp.where(lane == row + h * group + heads, total[part], packed[i])
        for i in range(chunk):
            stats[base + i] = jnp.sum(packed[i], axis=0, keepdims=True)

    @pl.loop(0, line)
    def _(step):
        base = (me ^ (step * chunk)) // chunk * chunk

        @pl.when(step == 1)
        def _():
            last_across()

        arrive(beside ^ (step * chunk))
        arrive(beside ^ 2 ^ (step * chunk))
        process(base)

        @pl.loop(0, chunk)
        def _(i):
            @pl.when(base + i != me)
            def _():
                stats_copy(base + i).start()
                sums_copy(base + i).start()

    stats_in[me] = stats[me]
    sums_in[me] = sums[me]

    @pl.loop(1, n)
    def _(step):
        peer = me ^ step
        pltpu.make_async_remote_copy(
            src_ref=stats.at[peer], dst_ref=stats_in.at[peer], send_sem=t_send.at[peer], recv_sem=t_recv.at[peer],
            device_id={"ctx": peer}, device_id_type=MESH).wait_recv()

    st = stats_in[...].reshape(n, width)
    coef = jnp.exp2((st - jnp.max(st, axis=0, keepdims=True)) * factor) * pltpu.roll(st, width - heads, 1)
    w = coef / jnp.sum(coef, axis=0, keepdims=True)
    if n < width:
        w = jnp.concatenate([w, jnp.zeros((width - n, width), jnp.float32)], axis=0)
    w = w.T

    @pl.loop(1, n)
    def _(step):
        peer = me ^ step
        pltpu.make_async_remote_copy(
            src_ref=sums.at[peer], dst_ref=sums_in.at[peer], send_sem=s_send.at[peer], recv_sem=s_recv.at[peer],
            device_id={"ctx": peer}, device_id_type=MESH).wait_recv()

    result = jnp.zeros((heads, width), jnp.float32)
    for b in range(n):
        result += w[:heads, b:b + 1] * sums_in[b].astype(jnp.float32)
    out_ref[...] = result.astype(jnp.bfloat16)

    @pl.loop(1, n)
    def _(step):
        peer = me ^ step
        stats_copy(peer).wait_send()
        sums_copy(peer).wait_send()

    @pl.loop(1, n)
    def _(slot):
        q_copy(me, beside, slot).wait_send()


def body(n, queries, fresh_keys, fresh_values, cache_keys, stored_values, cache_lengths, positions):
    rows = queries.shape[0]
    assert rows == 1
    heads = queries.shape[1] // HEAD_WIDTH
    cache_rows, kv_width = cache_keys.shape
    chunk = 4
    assert n & (n - 1) == 0 and n % chunk == 0 and 2 * heads <= HEAD_WIDTH
    block = (n, heads, HEAD_WIDTH)
    operands = (queries, fresh_keys, fresh_values, cache_keys, stored_values, cache_lengths, positions)
    dma = pltpu.SemaphoreType.DMA
    out = pl.pallas_call(
        functools.partial(kernel, n, chunk),
        out_shape=jax.ShapeDtypeStruct((heads, HEAD_WIDTH), jnp.bfloat16),
        in_specs=[pl.BlockSpec(memory_space=pl.ANY)] * len(operands),
        out_specs=pl.BlockSpec(memory_space=pltpu.VMEM),
        scratch_shapes=[
            pltpu.VMEM((cache_rows, kv_width), jnp.bfloat16),
            pltpu.VMEM((cache_rows, kv_width), jnp.bfloat16),
            pltpu.VMEM(queries.shape, jnp.bfloat16),
            pltpu.VMEM(fresh_keys.shape, jnp.bfloat16),
            pltpu.VMEM(fresh_values.shape, jnp.bfloat16),
            pltpu.SMEM(cache_lengths.shape, jnp.int32),
            pltpu.SMEM(positions.shape, jnp.int32),
            pltpu.VMEM(block, jnp.bfloat16),
            pltpu.VMEM(block, jnp.bfloat16),
            pltpu.VMEM((n, 1, HEAD_WIDTH), jnp.float32),
            pltpu.VMEM(block, jnp.bfloat16),
            pltpu.VMEM((n, 1, HEAD_WIDTH), jnp.float32),
            dma((len(operands),)), dma((n,)), dma((n,)), dma((n,)), dma((n,)), dma((n,)), dma((n,)),
        ],
        compiler_params=pltpu.CompilerParams(collective_id=0, has_side_effects=True),
    )(*operands)
    return out.reshape(rows, heads * HEAD_WIDTH)


def solution(mesh):
    return jax.shard_map(
        functools.partial(body, mesh.shape["ctx"]),
        mesh=mesh,
        in_specs=(
            P(("groups", "ctx"), None),
            P(("groups", "ctx"), None),
            P(("groups", "ctx"), None),
            P(("groups", "ctx"), None),
            P(("groups", "ctx"), None),
            P(("groups", "ctx")),
            P("groups"),
        ),
        out_specs=P(("groups", "ctx"), None),
        check_vma=False,
    )
```

time: 27 us -> 25.2 us (0.933)
  other arithmetic: 1.45 us -> 0 us
  Pallas kernels: 23.2 us -> 22.9 us
    unnamed x1 -> x0, other arithmetic: 1.45 us -> none
    pallas_call x1, Pallas kernels: 23.2 us -> 22.9 us  [body(): pl.pallas_call(functools.partial(kernel, n, chunk), out_shape=jax.ShapeDt...]
where the time goes in v2:
time: 25.2 us; the launch traced here: 24.9 us
  Pallas kernels  22.9 us (91%)
  local copies, waits for them, and re-layouts  1.36 us (5%)
  between operations  0.66 us (3%)
    pallas_call x1, Pallas kernels, body(): pl.pallas_call(functools.partial(kernel, n, chunk), out_shape=jax.ShapeDt...  22.9 us
    unnamed x1, local copies, waits for them, and re-layouts  1.36 us

profile of v2, /device:TPU:0, one launch (start us, length us, event | category | flops | bytes accessed | tf_op | source)
XLA Modules:
  0.0 24.9 jit_solution(18124876902816655439)
XLA Ops:
  0.7 22.9 %shard_map.73 = bf16[64,128]{1,0:T(8,128)(2,1)} custom-call(bf16[1,8192]{1,0:T(2,128)(2,1)} %queries_hbm.1, bf16[1,512]{1,0:T(2,128)(2,1)} %fresh_keys_hbm.1, bf16[1,512]{1,0:T(2,128)(2,1)} %fresh_values_hbm.1, bf16[1024,512]{1,0:T(8,128)(2,1)} %keys_hbm.1, bf16[1024,512]{1,0:T(8,128)(2,1)} %values_hbm.1, s32[1]{0:T(128)S(6)} %copy.11.lengths_hbm, ...), custom_call_target="tpu_custom_call" | custom-call | tf_op jit(solution)/shard_map/pallas_call | solution.py:207
  23.6 1.4 %copy.10 = bf16[1,1,64,128]{3,1,2,0:T(2,128)(2,1)} copy(bf16[1,1,64,128]{3,2,1,0:T(8,128)(2,1)} %bitcast.5) | data formatting | bytes 32768

commit v3 on v2

--- a/solution.py
+++ b/solution.py
@@ -25,7 +25,6 @@
     kv_heads = heads // group
     factor = width ** -0.5 * math.log2(math.e)
     line = n // chunk
-    beside, across = me ^ 1, me ^ 2
 
     loads = [
         pltpu.make_async_copy(src, dst, load_sem.at[i])
@@ -37,52 +36,23 @@
         load.start()
 
     barrier = pltpu.get_barrier_semaphore()
-    pl.semaphore_signal(barrier, inc=1, device_id={"ctx": beside}, device_id_type=MESH)
-    pl.semaphore_signal(barrier, inc=1, device_id={"ctx": across}, device_id_type=MESH)
-
-    @pl.loop(1, line)
-    def _(t):
-        pl.semaphore_signal(barrier, inc=1, device_id={"ctx": me ^ (t * chunk)}, device_id_type=MESH)
+
+    @pl.loop(1, n)
+    def _(step):
+        pl.semaphore_signal(barrier, inc=1, device_id={"ctx": me ^ step}, device_id_type=MESH)
 
     loads[0].wait()
     q_all[me] = q_row[...].astype(jnp.float32).reshape(heads, width).astype(jnp.bfloat16)
-    pl.semaphore_wait(barrier, line + 1)
-
-    def q_copy(row, peer, slot):
+    pl.semaphore_wait(barrier, n - 1)
+
+    def q_copy(row, peer):
         return pltpu.make_async_remote_copy(
-            src_ref=q_all.at[row], dst_ref=q_all.at[row], send_sem=q_send.at[slot], recv_sem=q_recv.at[row],
+            src_ref=q_all.at[row], dst_ref=q_all.at[row], send_sem=q_send.at[peer], recv_sem=q_recv.at[row],
             device_id={"ctx": peer}, device_id_type=MESH)
 
-    def to_line(t):
-        return q_copy(me, me ^ (t * chunk), t)
-
-    def to_across(t):
-        return q_copy(me ^ (t * chunk), across, line + t)
-
-    def to_beside(t, far):
-        return q_copy((across if far else me) ^ (t * chunk), beside, (2 + far) * line + t)
-
-    def arrive(row):
-        q_copy(row, beside, 0).wait_recv()
-
-    @pl.loop(1, line)
-    def _(t):
-        to_line(line - t).start()
-
-    to_across(0).start()
-    to_beside(0, 0).start()
-
-    @pl.loop(1, line)
-    def _(t):
-        arrive(me ^ (t * chunk))
-        to_across(t).start()
-        to_beside(t, 0).start()
-        arrive(across ^ ((t - 1) * chunk))
-        to_beside(t - 1, 1).start()
-
-    def last_across():
-        arrive(across ^ ((line - 1) * chunk))
-        to_beside(line - 1, 1).start()
+    @pl.loop(1, n)
+    def _(step):
+        q_copy(me, me ^ step).start()
 
     for load in loads[1:]:
         load.wait()
@@ -94,8 +64,6 @@
     row = lax.broadcasted_iota(jnp.int32, (group, width), 0)
     ones = jnp.ones((cache_rows, width), jnp.bfloat16)
     own_order = positions_ref[me]
-    if line == 1:
-        last_across()
 
     def sums_copy(peer):
         return pltpu.make_async_remote_copy(
@@ -139,12 +107,12 @@
     def _(step):
         base = (me ^ (step * chunk)) // chunk * chunk
 
-        @pl.when(step == 1)
-        def _():
-            last_across()
-
-        arrive(beside ^ (step * chunk))
-        arrive(beside ^ 2 ^ (step * chunk))
+        @pl.loop(0, chunk)
+        def _(i):
+            @pl.when(base + i != me)
+            def _():
+                q_copy(base + i, base + i).wait_recv()
+
         process(base)
 
         @pl.loop(0, chunk)
@@ -188,10 +156,7 @@
         peer = me ^ step
         stats_copy(peer).wait_send()
         sums_copy(peer).wait_send()
-
-    @pl.loop(1, n)
-    def _(slot):
-        q_copy(me, beside, slot).wait_send()
+        q_copy(me, peer).wait_send()
 
 
 def body(n, queries, fresh_keys, fresh_values, cache_keys, stored_values, cache_lengths, positions):

time: 25.2 us -> 23.4 us (0.929)
  Pallas kernels: 22.9 us -> 21.2 us
    pallas_call x1, Pallas kernels: 22.9 us -> 21.2 us  [body(): pl.pallas_call(functools.partial(kernel, n, chunk), out_shape=jax.ShapeDt...]
where the time goes in v3:
time: 23.4 us; the launch traced here: 23.2 us
  Pallas kernels  21.2 us (91%)
  local copies, waits for them, and re-layouts  1.36 us (6%)
  between operations  0.66 us (3%)
    pallas_call x1, Pallas kernels, body(): pl.pallas_call(functools.partial(kernel, n, chunk), out_shape=jax.ShapeDt...  21.2 us
    unnamed x1, local copies, waits for them, and re-layouts  1.36 us

profile of v3, /device:TPU:0, one launch (start us, length us, event | category | flops | bytes accessed | tf_op | source)
XLA Modules:
  0.0 23.2 jit_solution(13729785571464163753)
XLA Ops:
  0.7 21.2 %shard_map.73 = bf16[64,128]{1,0:T(8,128)(2,1)} custom-call(bf16[1,8192]{1,0:T(2,128)(2,1)} %queries_hbm.1, bf16[1,512]{1,0:T(2,128)(2,1)} %fresh_keys_hbm.1, bf16[1,512]{1,0:T(2,128)(2,1)} %fresh_values_hbm.1, bf16[1024,512]{1,0:T(8,128)(2,1)} %keys_hbm.1, bf16[1024,512]{1,0:T(8,128)(2,1)} %values_hbm.1, s32[1]{0:T(128)S(6)} %copy.11.lengths_hbm, ...), custom_call_target="tpu_custom_call" | custom-call | tf_op jit(solution)/shard_map/pallas_call | solution.py:172
  21.8 1.4 %copy.10 = bf16[1,1,64,128]{3,1,2,0:T(2,128)(2,1)} copy(bf16[1,1,64,128]{3,2,1,0:T(8,128)(2,1)} %bitcast.5) | data formatting | bytes 32768

commit v4 on v3

--- a/solution.py
+++ b/solution.py
@@ -47,7 +47,7 @@
 
     def q_copy(row, peer):
         return pltpu.make_async_remote_copy(
-            src_ref=q_all.at[row], dst_ref=q_all.at[row], send_sem=q_send.at[peer], recv_sem=q_recv.at[row],
+            src_ref=q_all.at[row], dst_ref=q_all.at[row], send_sem=q_send.at[0], recv_sem=q_recv.at[row],
             device_id={"ctx": peer}, device_id_type=MESH)
 
     @pl.loop(1, n)
@@ -67,12 +67,12 @@
 
     def sums_copy(peer):
         return pltpu.make_async_remote_copy(
-            src_ref=sums.at[peer], dst_ref=sums_in.at[me], send_sem=s_send.at[peer], recv_sem=s_recv.at[me],
+            src_ref=sums.at[peer], dst_ref=sums_in.at[me], send_sem=s_send.at[0], recv_sem=s_recv.at[0],
             device_id={"ctx": peer}, device_id_type=MESH)
 
     def stats_copy(peer):
         return pltpu.make_async_remote_copy(
-            src_ref=stats.at[peer], dst_ref=stats_in.at[me], send_sem=t_send.at[peer], recv_sem=t_recv.at[me],
+            src_ref=stats.at[peer], dst_ref=stats_in.at[me], send_sem=t_send.at[0], recv_sem=t_recv.at[0],
             device_id={"ctx": peer}, device_id_type=MESH)
 
     def process(base):
@@ -125,12 +125,14 @@
     stats_in[me] = stats[me]
     sums_in[me] = sums[me]
 
-    @pl.loop(1, n)
-    def _(step):
-        peer = me ^ step
-        pltpu.make_async_remote_copy(
-            src_ref=stats.at[peer], dst_ref=stats_in.at[peer], send_sem=t_send.at[peer], recv_sem=t_recv.at[peer],
-            device_id={"ctx": peer}, device_id_type=MESH).wait_recv()
+    others = pl.ds(0, n - 1)
+
+    def all_of(src, dst, send, recv):
+        return pltpu.make_async_remote_copy(
+            src_ref=src.at[others], dst_ref=dst.at[others], send_sem=send.at[0], recv_sem=recv.at[0],
+            device_id={"ctx": me ^ 1}, device_id_type=MESH)
+
+    all_of(stats, stats_in, t_send, t_recv).wait_recv()
 
     st = stats_in[...].reshape(n, width)
     coef = jnp.exp2((st - jnp.max(st, axis=0, keepdims=True)) * factor) * pltpu.roll(st, width - heads, 1)
@@ -139,24 +141,16 @@
         w = jnp.concatenate([w, jnp.zeros((width - n, width), jnp.float32)], axis=0)
     w = w.T
 
-    @pl.loop(1, n)
-    def _(step):
-        peer = me ^ step
-        pltpu.make_async_remote_copy(
-            src_ref=sums.at[peer], dst_ref=sums_in.at[peer], send_sem=s_send.at[peer], recv_sem=s_recv.at[peer],
-            device_id={"ctx": peer}, device_id_type=MESH).wait_recv()
+    all_of(sums, sums_in, s_send, s_recv).wait_recv()
 
     result = jnp.zeros((heads, width), jnp.float32)
     for b in range(n):
         result += w[:heads, b:b + 1] * sums_in[b].astype(jnp.float32)
     out_ref[...] = result.astype(jnp.bfloat16)
 
-    @pl.loop(1, n)
-    def _(step):
-        peer = me ^ step
-        stats_copy(peer).wait_send()
-        sums_copy(peer).wait_send()
-        q_copy(me, peer).wait_send()
+    all_of(stats, stats_in, t_send, t_recv).wait_send()
+    all_of(sums, sums_in, s_send, s_recv).wait_send()
+    all_of(q_all, q_all, q_send, q_recv).wait_send()
 
 
 def body(n, queries, fresh_keys, fresh_values, cache_keys, stored_values, cache_lengths, positions):
@@ -187,7 +181,7 @@
             pltpu.VMEM((n, 1, HEAD_WIDTH), jnp.float32),
             pltpu.VMEM(block, jnp.bfloat16),
             pltpu.VMEM((n, 1, HEAD_WIDTH), jnp.float32),
-            dma((len(operands),)), dma((n,)), dma((n,)), dma((n,)), dma((n,)), dma((n,)), dma((n,)),
+            dma((len(operands),)), dma((1,)), dma((n,)), dma((1,)), dma((1,)), dma((1,)), dma((1,)),
         ],
         compiler_params=pltpu.CompilerParams(collective_id=0, has_side_effects=True),
     )(*operands)

time: 23.4 us -> 22.6 us (0.966)
  Pallas kernels: 21.2 us -> 20.3 us
    pallas_call x1, Pallas kernels: 21.2 us -> 20.3 us  [body(): pl.pallas_call(functools.partial(kernel, n, chunk), out_shape=jax.ShapeDt...]
where the time goes in v4:
time: 22.6 us; the launch traced here: 22.3 us
  Pallas kernels  20.3 us (90%)
  local copies, waits for them, and re-layouts  1.36 us (6%)
  between operations  0.66 us (3%)
    pallas_call x1, Pallas kernels, body(): pl.pallas_call(functools.partial(kernel, n, chunk), out_shape=jax.ShapeDt...  20.3 us
    unnamed x1, local copies, waits for them, and re-layouts  1.36 us

profile of v4, /device:TPU:0, one launch (start us, length us, event | category | flops | bytes accessed | tf_op | source)
XLA Modules:
  0.0 22.3 jit_solution(1693797007821297184)
XLA Ops:
  0.7 20.3 %shard_map.73 = bf16[64,128]{1,0:T(8,128)(2,1)} custom-call(bf16[1,8192]{1,0:T(2,128)(2,1)} %queries_hbm.1, bf16[1,512]{1,0:T(2,128)(2,1)} %fresh_keys_hbm.1, bf16[1,512]{1,0:T(2,128)(2,1)} %fresh_values_hbm.1, bf16[1024,512]{1,0:T(8,128)(2,1)} %keys_hbm.1, bf16[1024,512]{1,0:T(8,128)(2,1)} %values_hbm.1, s32[1]{0:T(128)S(6)} %copy.11.lengths_hbm, ...), custom_call_target="tpu_custom_call" | custom-call | tf_op jit(solution)/shard_map/pallas_call | solution.py:166
  21.0 1.4 %copy.10 = bf16[1,1,64,128]{3,1,2,0:T(2,128)(2,1)} copy(bf16[1,1,64,128]{3,2,1,0:T(8,128)(2,1)} %bitcast.5) | data formatting | bytes 32768
